TPU v7x, 32 devices: a whole 2x2x4 slice. The times are simulated.
32 devices in a mesh: leaf: 4 (over x, core), front: 8 (over z, y), wave: 1.
Axes of the slice: x: 2, y: 2, z: 4, core: 2. Of those that a mesh axis runs over, the one named last changes fastest.
Arguments:
- sources: float32 [8192, 128], P(('wave', 'front')), may hold values from -48 to 48
- order: int32 [8192], P('front'), may hold values from 0 to 8191, as said below
- diagonal: float32 [8192], P(('wave', 'front')), may hold values from 0.1 to 2
- coupling: float32 [8192, 4096], P(('wave', 'front'), 'leaf'), may hold values from -0.0625 to 0.0625
- interior_inverse: float32 [64, 64, 64], P(('wave', 'leaf')), may hold values from -2 to 6, as said below
- interior_load: float32 [64, 64, 128], P(('wave', 'leaf')), may hold values from -6 to 6
Outputs:
- solution: float32 [8192, 128], P(('wave', 'front'))
- interior_solution: float32 [64, 64, 128], P(('wave', 'leaf'))
Inputs may be any that keep to these rules, and one draw needn't show every extreme that they name: `order`: each aligned block of 1024 entries is a permutation of that block's own indices. `interior_inverse`: each matrix is symmetric positive definite.
All inputs are finite; a program needn't handle non-finite values.
Results may differ from a plain program's by a relative error of at most 0.0003.
Values sent between devices are 32-bit elements; how exact they have to be, the bound alone decides.
No kernel may reach another device: no remote copies, remote signals or barrier semaphores. Data moves between devices by JAX's collectives and lax.ppermute only.
A program may use at most 64 MiB of HBM per device.

v0:
```python
import jax
import jax.numpy as jnp
from jax import lax
from jax.sharding import PartitionSpec as P

ITERS = 4


HIGHEST = lax.Precision.HIGHEST


def couple(coupling, field):
    partial_sums = jnp.einsum("sk,sn->kn", coupling, field, precision=HIGHEST)
    return lax.psum(partial_sums, "front")


def condense(interior_inverse, projected):
    shaped = projected.reshape(
        interior_inverse.shape[0], interior_inverse.shape[1], projected.shape[1]
    )
    return jnp.einsum("bij,bjn->bin", interior_inverse, shaped, precision=HIGHEST)


def cg_update(solution, residual, direction, image, norm_now, own):
    mine_dir = own(direction)
    mine_res = own(residual)
    mine_img = own(image)
    curvature, cross, square = lax.psum(
        (
            jnp.sum(mine_dir * mine_img, axis=0),
            jnp.sum(mine_res * mine_img, axis=0),
            jnp.sum(mine_img * mine_img, axis=0),
        ),
        ("leaf", "front"),
    )
    step_size = norm_now / curvature
    norm_next = norm_now - 2.0 * step_size * cross + step_size * step_size * square
    solution = solution + step_size * direction
    residual = residual - step_size * image
    direction = residual + norm_next / norm_now * direction
    return (solution, residual, direction, norm_next)


def per_device(sources, order, diagonal, coupling, interior_inverse, interior_load):
    rows_here = sources.shape[0]
    columns = sources.shape[1]
    positions = order - lax.axis_index("front") * rows_here
    loads = jnp.take(sources, positions, axis=0)
    share_rows = rows_here // lax.axis_size("leaf")
    first_row = lax.axis_index("leaf") * share_rows

    def own_rows(field):
        return lax.dynamic_slice_in_dim(field, first_row, share_rows, 0)

    start_share = own_rows(loads)
    start_total = lax.psum(jnp.sum(start_share * start_share, axis=0), ("leaf", "front"))
    solution = jnp.zeros_like(loads)
    residual = loads
    direction = loads
    norm_now = start_total
    for iteration in range(ITERS):
        coeffs = condense(interior_inverse, couple(coupling, direction)).reshape(-1, columns)
        spread_term = jnp.einsum("sk,kn->sn", coupling, coeffs, precision=HIGHEST)
        image = diagonal[:, None] * direction + lax.psum(spread_term, "leaf")
        solution, residual, direction, norm_now = cg_update(
            solution, residual, direction, image, norm_now, own_rows
        )
    projected = couple(coupling, solution).reshape(interior_load.shape)
    interior_solution = jnp.einsum(
        "bij,bjn->bin", interior_inverse, interior_load - projected, precision=HIGHEST
    )
    return (solution, interior_solution)


def solution(mesh):
    return jax.shard_map(
        per_device,
        mesh=mesh,
        in_specs=(
            P(("wave", "front"), None),
            P("front"),
            P(("wave", "front")),
            P(("wave", "front"), "leaf"),
            P(("wave", "leaf"), None, None),
            P(("wave", "leaf"), None, None),
        ),
        out_specs=(P(("wave", "front"), None), P(("wave", "leaf"), None, None)),
        check_vma=False,
    )
```

profile of v0, /device:TPU:0, one launch (start us, length us, event | category | flops | bytes accessed | tf_op | source)
XLA Modules:
  0.0 752.2 jit_solution(4193403296460094578)
XLA Ops:
  8.7 3.8 gather_fusion
  12.8 4.6 convolution_bitcast_fusion.9
  18.4 75.5 %all-reduce.13.cloned.1.call-done = f32[16,64,128]{2,1,0:T(8,128)} async-done(((f32[16,64,128]{2,1,0:T(8,128)}), f32[16,64,128]{2,1,0:T(8,128)}) %all-reduce.13.cloned.1.call-update) | async-done | bytes 524304 | tf_op jit(solution)/shard_map/psum | solution.py:14
  94.0 1.7 fusion.7
  95.7 7.5 %convolution_bitcast_fusion.8 = f32[1024,128]{0,1:T(8,128)} fusion(f32[1024,128]{1,0:T(8,128)S(1)} %bitcast.64, f32[1024,1024]{1,0:T(8,128)} %param.9), kind=kOutput, calls=%fused_computation.9 | convolution fusion | flops 1610612736 | bytes 5242880 | tf_op jit(solution)/shard_map/sk,kn->sn/dot_general | solution.py:63
  103.3 32.7 %all-reduce.15.cloned.1.call-done = f32[1024,128]{0,1:T(8,128)} async-done(((f32[1024,128]{0,1:T(8,128)}), f32[1024,128]{0,1:T(8,128)}) %all-reduce.15.cloned.1.call-update) | async-done | bytes 524304 | tf_op jit(solution)/shard_map/psum | solution.py:64
  136.0 1.1 multiply_add_fusion.6
  137.3 39.5 %all-reduce.2 = (f32[128]{0:T(128)S(1)}, f32[128]{0:T(128)S(1)}, f32[128]{0:T(128)S(1)}) all-reduce(f32[128]{0:T(128)S(1)} %get-tuple-element.14, f32[128]{0:T(128)S(1)} %get-tuple-element.13, f32[128]{0:T(128)S(1)} %get-tuple-element.12), channel_id=1, replica_groups=mesh['leaf'=4,'front'=8,'wave'=1] {'leaf','front'}, use_global_device_ids=true, to_apply=%region_1.2 | all-reduce | flops 384 | bytes 3072 | tf_op jit(solution)/shard_map/psum | solution.py:56
  176.9 4.6 convolution_bitcast_fusion.7
  182.8 73.2 %all-reduce.17.cloned.1.call-done = f32[16,64,128]{2,1,0:T(8,128)} async-done(((f32[16,64,128]{2,1,0:T(8,128)}), f32[16,64,128]{2,1,0:T(8,128)}) %all-reduce.17.cloned.1.call-update) | async-done | bytes 524304 | tf_op jit(solution)/shard_map/psum | solution.py:14
  255.9 1.7 fusion.8
  257.6 7.5 convolution_bitcast_fusion.6
  265.1 32.7 %all-reduce.19.cloned.1.call-done = f32[1024,128]{0,1:T(8,128)} async-done(((f32[1024,128]{0,1:T(8,128)}), f32[1024,128]{0,1:T(8,128)}) %all-reduce.19.cloned.1.call-update) | async-done | bytes 524304 | tf_op jit(solution)/shard_map/psum | solution.py:64
  297.8 1.1 multiply_add_fusion.4
  299.1 39.5 %all-reduce.1 = (f32[128]{0:T(128)S(1)}, f32[128]{0:T(128)S(1)}, f32[128]{0:T(128)S(1)}) all-reduce(f32[128]{0:T(128)S(1)} %get-tuple-element.11, f32[128]{0:T(128)S(1)} %get-tuple-element.10, f32[128]{0:T(128)S(1)} %get-tuple-element.9), channel_id=1, replica_groups=mesh['leaf'=4,'front'=8,'wave'=1] {'leaf','front'}, use_global_device_ids=true, to_apply=%region_11.12 | all-reduce | flops 384 | bytes 3072 | tf_op jit(solution)/shard_map/psum | solution.py:28
  339.5 4.6 convolution_bitcast_fusion.5
  345.4 73.1 %all-reduce.21.cloned.1.call-done = f32[16,64,128]{2,1,0:T(8,128)} async-done(((f32[16,64,128]{2,1,0:T(8,128)}), f32[16,64,128]{2,1,0:T(8,128)}) %all-reduce.21.cloned.1.call-update) | async-done | bytes 524304 | tf_op jit(solution)/shard_map/psum | solution.py:14
  418.5 1.7 fusion.9
  420.2 7.5 convolution_bitcast_fusion.4
  427.7 32.7 %all-reduce.23.cloned.1.call-done = f32[1024,128]{0,1:T(8,128)} async-done(((f32[1024,128]{0,1:T(8,128)}), f32[1024,128]{0,1:T(8,128)}) %all-reduce.23.cloned.1.call-update) | async-done | bytes 524304 | tf_op jit(solution)/shard_map/psum | solution.py:64
  460.4 1.1 multiply_add_fusion.2
  461.7 39.5 %all-reduce = (f32[128]{0:T(128)S(1)}, f32[128]{0:T(128)S(1)}, f32[128]{0:T(128)S(1)}) all-reduce(f32[128]{0:T(128)S(1)} %get-tuple-element.7, f32[128]{0:T(128)S(1)} %get-tuple-element.8, f32[128]{0:T(128)S(1)} %get-tuple-element.6), channel_id=1, replica_groups=mesh['leaf'=4,'front'=8,'wave'=1] {'leaf','front'}, use_global_device_ids=true, to_apply=%region_23.24 | all-reduce | flops 384 | bytes 3072 | tf_op jit(solution)/shard_map/psum | solution.py:28
  501.2 1.2 multiply_add_fusion.1
  502.4 4.6 convolution_bitcast_fusion.3
  508.4 73.1 %all-reduce.25.cloned.1.call-done = f32[16,64,128]{2,1,0:T(8,128)} async-done(((f32[16,64,128]{2,1,0:T(8,128)}), f32[16,64,128]{2,1,0:T(8,128)}) %all-reduce.25.cloned.1.call-update) | async-done | bytes 524304 | tf_op jit(solution)/shard_map/psum | solution.py:14
  581.4 1.7 fusion.10
  583.1 7.5 %convolution_bitcast_fusion.2 = f32[1024,128]{0,1:T(8,128)} fusion(f32[1024,128]{1,0:T(8,128)S(1)} %bitcast.67, f32[1024,1024]{1,0:T(8,128)} %param.9), kind=kOutput, calls=%fused_computation.3 | convolution fusion | flops 1610612736 | bytes 5242880 | tf_op jit(solution)/shard_map/sk,kn->sn/dot_general | solution.py:63
  590.8 32.6 %all-reduce.27.cloned.1.call-done = f32[1024,128]{0,1:T(8,128)} async-done(((f32[1024,128]{0,1:T(8,128)}), f32[1024,128]{0,1:T(8,128)}) %all-reduce.27.cloned.1.call-update) | async-done | bytes 524304 | tf_op jit(solution)/shard_map/psum | solution.py:64
  624.4 39.4 %psum.153 = f32[128]{0:T(128)S(1)} all-reduce(f32[128]{0:T(128)S(1)} %fusion.2), channel_id=1, replica_groups=mesh['leaf'=4,'front'=8,'wave'=1] {'leaf','front'}, use_global_device_ids=true, to_apply=%region_27.28 | all-reduce | flops 128 | bytes 1024 | tf_op jit(solution)/shard_map/psum | solution.py:28
  664.1 4.6 convolution_bitcast_fusion.1
  670.8 72.4 %all-reduce.29.cloned.1.call-done = f32[16,64,128]{2,1,0:T(8,128)} async-done(((f32[16,64,128]{2,1,0:T(8,128)}), f32[16,64,128]{2,1,0:T(8,128)}) %all-reduce.29.cloned.1.call-update) | async-done | bytes 524304 | tf_op jit(solution)/shard_map/psum | solution.py:14
  743.2 2.5 convolution_bitcast_fusion
  (48 shorter events, 11.8 us)
Async XLA Ops:
  7.2 86.8 %copy-start = (f32[16,64,64]{2,1,0:T(8,128)S(1)}, f32[16,64,64]{2,1,0:T(8,128)}, u32[]{:S(2)}) copy-start(f32[16,64,64]{2,1,0:T(8,128)} %param.10) | copy-start | bytes 786436
  7.2 86.8 %all-reduce.13.cloned.1.call-start = ((), (), s32[]{:S(2)}) async-start(), calls=%async_computation | async-start | bytes 1048576 | tf_op jit(solution)/shard_map/psum | solution.py:14
  18.4 117.6 %copy-start.3 = (f32[1024]{0:T(1024)S(1)}, f32[1024]{0:T(1024)}, u32[]{:S(2)}) copy-start(f32[1024]{0:T(1024)} %param.8) | copy-start | bytes 12292
  18.4 117.6 %all-reduce.15.cloned.1.call-start = ((), (), s32[]{:S(2)}) async-start(), calls=%async_computation.1 | async-start | bytes 1048576 | tf_op jit(solution)/shard_map/psum | solution.py:64
  103.2 152.7 %all-reduce.17.cloned.1.call-start = ((), (), s32[]{:S(2)}) async-start(), calls=%async_computation.2 | async-start | bytes 1048576 | tf_op jit(solution)/shard_map/psum | solution.py:14
  182.5 115.3 %all-reduce.19.cloned.1.call-start = ((), (), s32[]{:S(2)}) async-start(), calls=%async_computation.3 | async-start | bytes 1048576 | tf_op jit(solution)/shard_map/psum | solution.py:64
  265.1 153.5 %all-reduce.21.cloned.1.call-start = ((), (), s32[]{:S(2)}) async-start(), calls=%async_computation.4 | async-start | bytes 1048576 | tf_op jit(solution)/shard_map/psum | solution.py:14
  345.1 116.4 %copy-start.1 = (f32[1024,128]{0,1:T(8,128)S(1)}, f32[1024,128]{0,1:T(8,128)}, u32[]{:S(2)}) copy-start(f32[1024,128]{0,1:T(8,128)} %get-tuple-element.28) | copy-start | bytes 1572868
  345.1 115.3 %all-reduce.23.cloned.1.call-start = ((), (), s32[]{:S(2)}) async-start(), calls=%async_computation.5 | async-start | bytes 1048576 | tf_op jit(solution)/shard_map/psum | solution.py:64
  427.7 153.7 %all-reduce.25.cloned.1.call-start = ((), (), s32[]{:S(2)}) async-start(), calls=%async_computation.6 | async-start | bytes 1048576 | tf_op jit(solution)/shard_map/psum | solution.py:14
  508.0 115.4 %all-reduce.27.cloned.1.call-start = ((), (), s32[]{:S(2)}) async-start(), calls=%async_computation.7 | async-start | bytes 1048576 | tf_op jit(solution)/shard_map/psum | solution.py:64
  590.7 152.5 %all-reduce.29.cloned.1.call-start = ((), (), s32[]{:S(2)}) async-start(), calls=%async_computation.8 | async-start | bytes 1048576 | tf_op jit(solution)/shard_map/psum | solution.py:14
  664.1 79.1 %copy-start.2 = (f32[16,64,128]{2,1,0:T(8,128)S(1)}, f32[16,64,128]{2,1,0:T(8,128)}, u32[]{:S(2)}) copy-start(f32[16,64,128]{2,1,0:T(8,128)} %param.11) | copy-start | bytes 1572868
Sparse Core Ops, SparseCore 0:
  18.5 75.4 all-reduce.12
  103.3 32.5 all-reduce.14
  182.6 73.2 all-reduce.16
  265.2 32.5 all-reduce.18
  345.3 73.2 all-reduce.20
  427.8 32.5 all-reduce.22
  508.2 73.2 all-reduce.24
  590.8 32.5 all-reduce.26
  669.9 73.2 all-reduce.28
where the time goes:
time: 753 us; the launch traced here: 752 us
  waiting for transfers between devices  498 us (66%)
  blocking collectives  158 us (21%)
  matrix products  62.1 us (8%)
  between operations  14 us (2%)
  local copies, waits for them, and re-layouts  10.1 us (1%)
  other arithmetic  8.92 us (1%)
    psum x5, waiting for transfers between devices, couple(): return lax.psum(partial_sums, 'front')  367 us
    psum x4, waiting for transfers between devices, per_device(): image = diagonal[:, None] * direction + lax.psum(spread_term, 'leaf')  131 us
    psum x3, blocking collectives, cg_update(): lax.psum((jnp.sum(mine_dir * mine_img, axis=0), jnp.sum(mine_res * mine_i...  118 us
    psum x1, blocking collectives, per_device(): lax.psum(jnp.sum(start_share * start_share, axis=0), ('leaf', 'front'))  39.5 us
    dot_general x4, matrix products, per_device(): spread_term = jnp.einsum('sk,kn->sn', coupling, coeffs, precision=HIGHEST)  30 us
    dot_general x5, matrix products, couple(): partial_sums = jnp.einsum('sk,sn->kn', coupling, field, precision=HIGHEST)  23 us
  transfers between devices with their start and end apart: 9, of which 9 were waited for; matrix products, arithmetic and copies ran while one was open for 0% of the time, Pallas kernels for 0%

commit v1 on v0

v1 whole, which is shorter than its diff:
```python
import functools
import math

import jax
import jax.numpy as jnp
from jax import lax
from jax.experimental import pallas as pl
from jax.experimental.pallas import tpu as pltpu
from jax.sharding import PartitionSpec as P


ITERS = 4
GROUPS = 2
EXTRA = 8
LANES = 128
GRANT = 24 << 20
F32, BF16 = jnp.float32, jnp.bfloat16
AXES = ("leaf", "front", "wave")


def halves_of(value):
    high = value.astype(BF16)
    return high, (value - high.astype(F32)).astype(BF16)


def stacked(value):
    return jnp.concatenate(halves_of(value), axis=0)


def product(left, high, low):
    rows = left.shape[0] // 2
    whole = jnp.dot(left, high, preferred_element_type=F32)
    return whole[:rows] + whole[rows:] + jnp.dot(left[:rows], low, preferred_element_type=F32)


def as_rows(columns, width):
    sources = columns[0].shape[0]
    lane = lax.broadcasted_iota(jnp.int32, (sources, LANES), 1)
    table = jnp.zeros((sources, LANES), F32)
    for at, column in enumerate(columns):
        table = jnp.where(lane == at, column, table)
    turned = table.T[:EXTRA, :]
    return jnp.concatenate([turned, jnp.zeros((EXTRA, width - sources), F32)], axis=1)


def as_columns(rows, sources):
    block = jnp.concatenate([rows[:, :LANES], jnp.zeros((LANES - EXTRA, LANES), F32)], axis=0)
    return block.T[:sources, :]


def total_of(value):
    return jnp.sum(value, axis=1, keepdims=True)


def quarter_here():
    return lax.rem(lax.axis_index("front"), 4)


def core_here():
    return lax.rem(lax.axis_index("leaf"), 2)


def call(kernel, outs, *operands, scratch=(), flops=0, apart=(), grant=24 << 20):
    vmem = pl.BlockSpec(memory_space=pltpu.VMEM)
    anywhere = pl.BlockSpec(memory_space=pltpu.HBM)
    moved = sum(math.prod(shape) * jnp.dtype(dtype).itemsize for shape, dtype in outs)
    moved += sum(operand.size * operand.dtype.itemsize for operand in operands + tuple(apart))
    return pl.pallas_call(
        kernel,
        out_shape=[jax.ShapeDtypeStruct(shape, dtype) for shape, dtype in outs],
        in_specs=[anywhere] * len(apart) + [vmem] * len(operands),
        out_specs=[vmem] * len(outs),
        scratch_shapes=list(scratch),
        cost_estimate=pl.CostEstimate(flops=flops, bytes_accessed=moved, transcendentals=0),
        compiler_params=pltpu.CompilerParams(vmem_limit_bytes=grant),
    )(*apart, *operands)


def blocks_kernel(inverse_ref, high_ref, low_ref):
    count, width, _ = high_ref.shape
    rank = inverse_ref.shape[1]
    each = width // rank
    high_ref[...] = jnp.zeros_like(high_ref)
    low_ref[...] = jnp.zeros_like(low_ref)
    for at in range(count):
        for i in range(each):
            own = pl.ds(i * rank, rank)
            high_ref[at, own, own], low_ref[at, own, own] = halves_of(inverse_ref[at * each + i].T)


def interior_kernel(load_ref, high_ref, low_ref, out_ref):
    count, width, _ = high_ref.shape
    for at in range(count):
        own = pl.ds(at * width, width)
        out_ref[:, own] = product(stacked(load_ref[own, :].T), high_ref[at], low_ref[at])


def turn_kernel(coupling_ref, high_ref, low_ref):
    rows = high_ref.shape[0]
    for part in range(8):
        own = pl.ds(part * (rows // 8), rows // 8)
        high_ref[own, :], low_ref[own, :] = halves_of(coupling_ref[:, own].T)


def write_messages(me, residual, scaled, direction_scaled, high_ref, low_ref, out_ref):
    sources, quarter = residual.shape[0], out_ref.shape[2]
    sums = [total_of(residual * residual), total_of(scaled * residual)]
    if direction_scaled is not None:
        sums.append(total_of(residual * direction_scaled))
    sums = as_rows(sums, quarter)
    left = stacked(residual)
    for q in range(4):
        own = pl.ds(q * quarter, quarter)
        out_ref[q ^ me, :sources, :] = product(left, high_ref[:, own], low_ref[:, own])
        out_ref[q ^ me, sources:, :] = sums


def start_kernel(
    sources_hbm, coupling_hbm, order_hbm, diagonal_hbm,
    loads_a_ref, loads_b_ref, high_ref, low_ref, scale_ref, out_ref,
    sources_ref, coupling_ref, gathered_ref, order_ref, sems, small_sems,
):
    listed = pltpu.make_async_copy(order_hbm, order_ref, small_sems.at[0])
    scaled = pltpu.make_async_copy(diagonal_hbm, scale_ref, small_sems.at[1])
    taken = pltpu.make_async_copy(sources_hbm, sources_ref, sems.at[0])
    rows, parts = high_ref.shape[0], coupling_ref.shape[0]
    each = rows // parts
    copies = [
        pltpu.make_async_copy(coupling_hbm.at[pl.ds(i * each, each), :], coupling_ref.at[i], sems.at[1 + i])
        for i in range(parts)
    ]
    listed.start()
    taken.start()
    scaled.start()
    for copy in copies:
        copy.start()
    listed.wait()
    taken.wait()
    base = lax.axis_index("front") * high_ref.shape[0]
    group = 16

    def body(step, _):
        for i in range(group):
            at = step * group + i
            gathered_ref[pl.ds(at, 1), :] = sources_ref[pl.ds(order_ref[at] - base, 1), :]
        return 0

    lax.fori_loop(0, rows // group, body, 0)
    loads = gathered_ref[...].T
    half = loads.shape[0] // 2
    loads_a_ref[...], loads_b_ref[...] = loads[:half], loads[half:]
    for i, copy in enumerate(copies):
        copy.wait()
        own = pl.ds(i * each, each)
        high_ref[own, :], low_ref[own, :] = halves_of(coupling_ref[i])
    first = loads[:half]
    scaled.wait()
    write_messages(quarter_here(), first, scale_ref[...] * first, None, high_ref, low_ref, out_ref)


def first_kernel(loads_ref, diagonal_ref, high_ref, low_ref, out_ref):
    loads = loads_ref[...]
    write_messages(quarter_here(), loads, diagonal_ref[...] * loads, None, high_ref, low_ref, out_ref)


def update_kernel(
    state_ref, own_ref, other_ref, residual_ref, direction_ref, diagonal_ref, high_ref, low_ref,
    next_ref, step_ref, out_ref,
):
    me, core = quarter_here(), core_here()
    sources, half = other_ref.shape
    energy = as_columns(own_ref[sources:, :], sources)[:, 0:1]
    step = state_ref[1, :, 0:1] / (state_ref[2, :, 0:1] + energy)
    step_ref[...] = jnp.broadcast_to(step, step_ref.shape)
    for part, ref in ((core, own_ref), (1 - core, other_ref)):
        own = pl.ds(pl.multiple_of(part * half, half), half)
        image = diagonal_ref[:, own] * direction_ref[:, own] + ref[:sources, :]
        next_ref[:, own] = residual_ref[:, own] - step * image
    residual = next_ref[...]
    diagonal = diagonal_ref[...]
    write_messages(me, residual, diagonal * residual, diagonal * direction_ref[...], high_ref, low_ref, out_ref)


def condense_kernel(first, joint, here_ref, came_ref, *refs):
    refs = list(refs)
    before_ref, last_ref = (None, None) if first else (refs.pop(0), refs.pop(0))
    held_ref = refs.pop(0) if joint else None
    high_ref, low_ref, projected_ref, state_ref, out_ref = refs
    me = quarter_here()
    sources, quarter = projected_ref.shape
    total = here_ref[...] + came_ref[...]
    sums = as_columns(total[sources:], sources)
    norm, weighted = sums[:, 0:1], sums[:, 1:2]
    projected = total[:sources]
    ratio = jnp.zeros_like(norm)
    if not first:
        ratio = norm / last_ref[1, :, 0:1]
        weighted = weighted + 2.0 * ratio * sums[:, 2:3] + ratio * ratio * last_ref[2, :, 0:1]
        projected = projected + ratio * before_ref[...]
    projected_ref[...] = projected
    for at, value in enumerate((ratio, norm, weighted)):
        state_ref[at] = jnp.broadcast_to(value, (sources, LANES))
    coeffs = product(stacked(projected), high_ref[me], low_ref[me])
    out_ref[:sources, :] = coeffs
    energy = as_rows([total_of(projected * coeffs)], quarter)
    if held_ref is not None:
        row = lax.broadcasted_iota(jnp.int32, energy.shape, 0)
        energy = jnp.where(row == 1, energy[0:1, :], held_ref[sources:, :])
    out_ref[sources:, :] = energy


def advance_kernel(first, state_ref, step_ref, residual_ref, direction_ref, *refs):
    refs = list(refs)
    pieces, refs = refs[:4], refs[4:]
    solution_in, gathered_in = (None, None) if first else (refs.pop(0), refs.pop(0))
    next_ref, solution_ref, gathered_ref = refs
    step = step_ref[:, 0:1]
    direction = direction_ref[...]
    gain = step * direction
    solution_ref[...] = gain if first else solution_in[...] + gain
    sources = direction.shape[0]
    for slot, ref in enumerate(pieces):
        gain = step * ref[:sources, :]
        gathered_ref[slot] = gain if first else gathered_in[slot] + gain
    next_ref[...] = residual_ref[...] + state_ref[0, :, 0:1] * direction


def spread_kernel(c0, c1, c2, c3, high_ref, low_ref, out_ref, left_ref):
    me, core = quarter_here(), core_here()
    sources, quarter = c0.shape[0] - EXTRA, c0.shape[1]
    pieces = (c0, c1, c2, c3)
    for slot, ref in enumerate(pieces):
        own = pl.ds(pl.multiple_of((me ^ slot) * quarter, quarter), quarter)
        left_ref[:, own] = stacked(ref[:sources, :])
    energy = c0[sources:, :] + c1[sources:, :] + c2[sources:, :] + c3[sources:, :]
    left = left_ref[...]
    half = high_ref.shape[1] // 2
    chunk = min(half, 256)
    for part in range(2):
        for at in range(0, half, chunk):
            own = pl.ds(part * half + at, chunk)
            out_ref[part ^ core, :sources, pl.ds(at, chunk)] = product(left, high_ref[:, own], low_ref[:, own])
        out_ref[part ^ core, sources:, :] = jnp.concatenate(
            [energy[:, :LANES], jnp.zeros((EXTRA, half - LANES), F32)], axis=1
        )


def finish_kernel(interior_ref, energy_ref, *refs):
    inputs, (solution_ref, out_ref, left_ref) = refs[:-3], refs[-3:]
    me = quarter_here()
    each = len(inputs) // GROUPS
    energies = as_columns(energy_ref[...], left_ref.shape[0] // GROUPS)
    found = []
    for group in range(GROUPS):
        state_ref, direction_ref, *pieces, solution_in, gathered_in = inputs[group * each:(group + 1) * each]
        sources, quarter = pieces[0].shape[0] - EXTRA, pieces[0].shape[1]
        energy = energies[:, group:group + 1]
        step = state_ref[1, :, 0:1] / (state_ref[2, :, 0:1] + energy)
        found.append(solution_in[...] + step * direction_ref[...])
        rows = pl.ds(group * sources, sources)
        for slot, ref in enumerate(pieces):
            own = pl.ds(pl.multiple_of((me ^ slot) * quarter, quarter), quarter)
            left_ref[rows, own] = interior_ref[rows, own] - (gathered_in[slot] + step * ref[:sources, :])
    solution_ref[...] = jnp.concatenate(found, axis=0).T
    out_ref[...] = left_ref[...].T


def solver(n_leaf, n_front):
    assert n_leaf & (n_leaf - 1) == 0 and n_front & (n_front - 1) == 0
    assert n_leaf >= 2 and n_front >= 4

    def swap(value, leaf_mask, front_mask):
        pairs = [
            (leaf * n_front + front, (leaf ^ leaf_mask) * n_front + (front ^ front_mask))
            for leaf in range(n_leaf)
            for front in range(n_front)
        ]
        return lax.ppermute(value, AXES, pairs)

    def over_leaf(value):
        mask = 2
        while mask < n_leaf:
            value = value + swap(value, mask, 0)
            mask *= 2
        return value

    def over_near(messages):
        here = messages[0]
        for slot in (3, 1, 2):
            here = here + swap(messages[slot], 0, slot)
        return here

    def over_far(here):
        mask = 4
        while mask * 2 < n_front:
            here = here + swap(here, 0, mask)
            mask *= 2
        return here, (swap(here, 0, mask) if mask < n_front else jnp.zeros_like(here))

    def gathered_from(own):
        others = {}
        for slot in (3, 1, 2):
            others[slot] = swap(own, 0, slot)
        return [own, others[1], others[2], others[3]]

    def per_device(sources, order, diagonal, coupling, interior_inverse, interior_load):
        rows, columns = sources.shape
        width = coupling.shape[1]
        quarter, half, each = width // 4, rows // 2, columns // GROUPS
        blocks, rank, _ = interior_inverse.shape
        field = ((each, rows), F32)
        message = ((each + EXTRA, quarter), F32)
        messages_of = ((4, each + EXTRA, quarter), F32)
        state_of = ((3, each, LANES), F32)
        work = 6 * rows * width * each

        parts = 8
        *loads, high, low, scale, messages = call(
            start_kernel, [field, field] + [((rows, width), BF16)] * 2 + [((1, rows), F32), messages_of],
            apart=(sources, coupling, order, diagonal.reshape(1, rows)), flops=work, grant=GRANT,
            scratch=[
                pltpu.VMEM((rows, columns), F32), pltpu.VMEM((parts, rows // parts, width), F32),
                pltpu.VMEM((rows, columns), F32), pltpu.SMEM((rows,), jnp.int32),
                pltpu.SemaphoreType.DMA((1 + parts,)), pltpu.SemaphoreType.DMA((2,)),
            ],
        )
        here = [over_near(messages)]
        (messages,) = call(first_kernel, [messages_of], loads[1], scale, high, low, flops=work)
        here.append(over_near(messages))
        back = call(turn_kernel, [((width, rows), BF16)] * 2, coupling)
        inverse = call(blocks_kernel, [((4, quarter, quarter), BF16)] * 2, interior_inverse)
        (interior,) = call(
            interior_kernel, [((columns, blocks * rank), F32)], interior_load.reshape(-1, columns), *inverse,
        )

        class Group:
            pass

        groups = []
        for n in range(GROUPS):
            g = Group()
            g.residual = g.direction = loads[n]
            g.here = here[n]
            g.step = g.state = g.projected = g.solution = g.gathered = g.coeffs = None
            groups.append(g)

        def iterate(g, iteration, held):
            first, last = iteration == 0, iteration == ITERS - 1
            before = () if first else (g.projected, g.state)
            g.projected, g.state, own = call(
                functools.partial(condense_kernel, first, held is not None),
                [((each, quarter), F32), state_of, message],
                *over_far(g.here), *before, *(() if held is None else (held,)), *inverse,
                flops=6 * quarter * quarter * each,
            )
            fresh = gathered_from(own)
            if not first:
                kept = () if iteration == 1 else (g.solution, g.gathered)
                g.direction, g.solution, g.gathered = call(
                    functools.partial(advance_kernel, iteration == 1), [field, field, ((4, each, quarter), F32)],
                    g.state, g.step, g.residual, g.direction, *g.coeffs, *kept,
                )
            g.coeffs = fresh
            if last:
                return own
            (spread,) = call(
                spread_kernel, [((2, each + EXTRA, half), F32)], *fresh, *back,
                scratch=[pltpu.VMEM((2 * each, width), BF16)], flops=work,
            )
            came = swap(spread[1], 1, 0)
            mine = over_leaf(spread[0] + came)
            other = swap(mine[:each], 1, 0)
            g.residual, g.step, messages = call(
                update_kernel, [field, ((each, LANES), F32), messages_of],
                g.state, mine, other, g.residual, g.direction, scale, high, low, flops=work,
            )
            g.here = over_near(messages)

        for iteration in range(ITERS):
            held = None
            for g in groups:
                held = iterate(g, iteration, held)
        energy = sum(one[each:, :LANES] for one in groups[-1].coeffs)
        energy = over_leaf(energy + swap(energy, 1, 0))
        ends = []
        for g in groups:
            ends += [g.state, g.direction, *g.coeffs, g.solution, g.gathered]
        solution, interior = call(
            finish_kernel, [((rows, columns), F32), ((blocks * rank, columns), F32)], interior, energy, *ends,
            scratch=[pltpu.VMEM((columns, blocks * rank), F32)],
        )
        return solution, interior.reshape(interior_load.shape)

    return per_device


def solution(mesh):
    return jax.shard_map(
        solver(mesh.shape["leaf"], mesh.shape["front"]),
        mesh=mesh,
        in_specs=(
            P(("wave", "front"), None),
            P("front"),
            P(("wave", "front")),
            P(("wave", "front"), "leaf"),
            P(("wave", "leaf"), None, None),
            P(("wave", "leaf"), None, None),
        ),
        out_specs=(P(("wave", "front"), None), P(("wave", "leaf"), None, None)),
        check_vma=False,
    )
```

time: 753 us -> 161 us (0.21)
  waiting for transfers between devices: 498 us -> 40.7 us
  blocking collectives: 158 us -> 0 us
  starting transfers between devices: 1.04 us -> 89.6 us
  matrix products: 62.1 us -> 0 us
  Pallas kernels: 0 us -> 24 us
  between operations: 14 us -> 1.33 us
  other arithmetic: 8.92 us -> 0.47 us
    psum x9 -> x0, waiting for transfers between devices: 498 us -> none  [the longest x5 367 us: couple(): return lax.psum(partial_sums, 'front')]
    psum x4 -> x0, blocking collectives: 158 us -> none  [the longest x3 118 us: cg_update(): lax.psum((jnp.sum(mine_dir * mine_img, axis=0), jnp.sum(mine_res * mine_i...]
    ppermute x0 -> x76, starting transfers between devices: none -> 89.6 us  [swap(): return lax.ppermute(value, AXES, pairs)]
    dot_general x14 -> x0, matrix products: 62.1 us -> none  [the longest x4 30 us: per_device(): spread_term = jnp.einsum('sk,kn->sn', coupling, coeffs, precision=HIGHEST)]
    ppermute x0 -> x76, waiting for transfers between devices: none -> 40.7 us  [swap(): return lax.ppermute(value, AXES, pairs)]
    pallas_call x0 -> x32, Pallas kernels: none -> 24 us  [call(): pl.pallas_call(kernel, out_shape=[jax.ShapeDtypeStruct(shape, dtype) for...]
  transfers between devices with their start and end apart: 9 -> 76, of which waited for: 9 -> 25; matrix products, arithmetic and copies ran while one was open for 0% -> 0% of each run, Pallas kernels for 0% -> 11%
where the time goes in v1:
time: 161 us
  starting transfers between devices  89.6 us (56%)
  waiting for transfers between devices  40.7 us (25%)
  Pallas kernels  24 us (15%)
  local copies, waits for them, and re-layouts  4.88 us (3%)
    ppermute x76, starting transfers between devices, swap(): return lax.ppermute(value, AXES, pairs)  89.6 us
    ppermute x76, waiting for transfers between devices, swap(): return lax.ppermute(value, AXES, pairs)  40.7 us
    pallas_call x32, Pallas kernels, call(): pl.pallas_call(kernel, out_shape=[jax.ShapeDtypeStruct(shape, dtype) for...  24 us
    unnamed x14, local copies, waits for them, and re-layouts  4.61 us
  transfers between devices with their start and end apart: 76, of which 25 were waited for; matrix products, arithmetic and copies ran while one was open for 0% of the time, Pallas kernels for 11%

profile of v1, /device:TPU:0, one launch (start us, length us, event | category | flops | bytes accessed | tf_op | source)
XLA Modules:
  0.0 161.0 jit_solution(17371549744433567714)
XLA Ops:
  0.6 2.2 %copy-done = f32[1024,1024]{1,0:T(8,128)S(1)} copy-done((f32[1024,1024]{1,0:T(8,128)S(1)}, f32[1024,1024]{1,0:T(8,128)}, u32[]{:S(2)}) %copy-start) | copy-done | bytes 4194328
  5.2 3.8 %shard_map.79 = (f32[64,1024]{1,0:T(8,128)S(1)}, f32[64,1024]{1,0:T(8,128)S(1)}, bf16[1024,1024]{1,0:T(8,128)(2,1)S(1)}, bf16[1024,1024]{1,0:T(8,128)(2,1)S(1)},...) custom-call(f32[1024,128]{1,0:T(8,128)S(1)} %copy-done.2, f32[1024,1024]{1,0:T(8,128)S(1)} %copy-done, ...), custom_call_target="tpu_custom_call" | custom-call | flops 402653184 | bytes 9744384 | tf_op jit(solution)/shard_map/pallas_call | solution.py:68
  9.1 4.1 %collective-permute-start.34 = (f32[72,256]{1,0:T(8,128)S(1)}, f32[72,256]{1,0:T(8,128)S(1)}, u32[]{:S(2)}, u32[]{:S(2)}) collective-permute-start(f32[72,256]{1,0:T(8,128)S(1)} %get-tuple-element.151), channel_id=1, source_target_pairs={{0,3},{1,2},{2,1},{3,0},{4,7},{5,6},{6,5},{7,4},{8,11},{9,10},{10,... | collective-permute-start | bytes 221192 | tf_op jit(solution)/shard_map/ppermute | solution.py:278
  14.7 2.9 %collective-permute-start = (f32[72,256]{1,0:T(8,128)S(1)}, f32[72,256]{1,0:T(8,128)S(1)}, u32[]{:S(2)}, u32[]{:S(2)}) collective-permute-start(f32[72,256]{1,0:T(8,128)S(1)} %get-tuple-element.163), channel_id=1, source_target_pairs={{0,3},{1,2},{2,1},{3,0},{4,7},{5,6},{6,5},{7,4},{8,11},{9,10},{10,... | collective-permute-start | bytes 221192 | tf_op jit(solution)/shard_map/ppermute | solution.py:278
  18.8 3.0 %collective-permute-start.37 = (f32[72,256]{1,0:T(8,128)S(1)}, f32[72,256]{1,0:T(8,128)S(1)}, u32[]{:S(2)}, u32[]{:S(2)}) collective-permute-start(f32[72,256]{1,0:T(8,128)S(1)} %fusion.16.here_ref), channel_id=1, source_target_pairs={{0,4},{1,5},{2,6},{3,7},{4,0},{5,1},{6,2},{7,3},{8,12},{9,13},{10,... | collective-permute-start | bytes 221192 | tf_op jit(solution)/shard_map/ppermute | solution.py:278
  23.0 3.0 %collective-permute-start.3 = (f32[72,256]{1,0:T(8,128)S(1)}, f32[72,256]{1,0:T(8,128)S(1)}, u32[]{:S(2)}, u32[]{:S(2)}) collective-permute-start(f32[72,256]{1,0:T(8,128)S(1)} %fusion.8.here_ref), channel_id=1, source_target_pairs={{0,4},{1,5},{2,6},{3,7},{4,0},{5,1},{6,2},{7,3},{8,12},{9,13},{10,... | collective-permute-start | bytes 221192 | tf_op jit(solution)/shard_map/ppermute | solution.py:278
  27.8 1.5 collective-permute-start.39
  32.8 1.5 collective-permute-start.5
  37.2 2.4 %collective-permute-done.6.c3.refs_3_ = f32[72,256]{1,0:T(8,128)S(1)} collective-permute-done((f32[72,256]{1,0:T(8,128)S(1)}, f32[72,256]{1,0:T(8,128)S(1)}, u32[]{:S(2)}, u32[]{:S(2)}) %collective-permute-start.6) | collective-permute-done | bytes 73760 | tf_op jit(solution)/shard_map/ppermute | solution.py:278
  40.6 1.6 collective-permute-start.42
  43.5 3.9 %collective-permute-done.42 = f32[72,512]{1,0:T(8,128)S(1)} collective-permute-done((f32[72,512]{1,0:T(8,128)S(1)}, f32[72,512]{1,0:T(8,128)S(1)}, u32[]{:S(2)}, u32[]{:S(2)}) %collective-permute-start.42) | collective-permute-done | bytes 147488 | tf_op jit(solution)/shard_map/ppermute | solution.py:278
  47.5 2.6 %collective-permute-done.8 = f32[72,512]{1,0:T(8,128)S(1)} collective-permute-done((f32[72,512]{1,0:T(8,128)S(1)}, f32[72,512]{1,0:T(8,128)S(1)}, u32[]{:S(2)}, u32[]{:S(2)}) %collective-permute-start.8) | collective-permute-done | bytes 147488 | tf_op jit(solution)/shard_map/ppermute | solution.py:278
  59.3 3.5 %collective-permute-start.47 = (f32[72,256]{1,0:T(8,128)S(1)}, f32[72,256]{1,0:T(8,128)S(1)}, u32[]{:S(2)}, u32[]{:S(2)}) collective-permute-start(f32[72,256]{1,0:T(8,128)S(1)} %fusion.14.here_ref), channel_id=1, source_target_pairs={{0,4},{1,5},{2,6},{3,7},{4,0},{5,1},{6,2},{7,3},{8,12},{9,13},{10,... | collective-permute-start | bytes 221192 | tf_op jit(solution)/shard_map/ppermute | solution.py:278
  62.9 2.7 %collective-permute-start.13 = (f32[72,256]{1,0:T(8,128)S(1)}, f32[72,256]{1,0:T(8,128)S(1)}, u32[]{:S(2)}, u32[]{:S(2)}) collective-permute-start(f32[72,256]{1,0:T(8,128)S(1)} %fusion.22.here_ref), channel_id=1, source_target_pairs={{0,4},{1,5},{2,6},{3,7},{4,0},{5,1},{6,2},{7,3},{8,12},{9,13},{10,... | collective-permute-start | bytes 221192 | tf_op jit(solution)/shard_map/ppermute | solution.py:278
  68.5 2.6 %collective-permute-start.50 = (f32[72,256]{1,0:T(8,128)S(1)}, f32[72,256]{1,0:T(8,128)S(1)}, u32[]{:S(2)}, u32[]{:S(2)}) collective-permute-start(f32[72,256]{1,0:T(8,128)S(1)} %get-tuple-element.107.c0.refs_0_), channel_id=1, source_target_pairs={{0,3},{1,2},{2,1},{3,0},{4,7},{5,6},{6,5},{7,4},{8,11},{9,10},{10,... | collective-permute-start | bytes 221192 | tf_op jit(solution)/shard_map/ppermute | solution.py:278
  72.7 2.3 %collective-permute-start.16 = (f32[72,256]{1,0:T(8,128)S(1)}, f32[72,256]{1,0:T(8,128)S(1)}, u32[]{:S(2)}, u32[]{:S(2)}) collective-permute-start(f32[72,256]{1,0:T(8,128)S(1)} %get-tuple-element.85.c0.refs_0_), channel_id=1, source_target_pairs={{0,3},{1,2},{2,1},{3,0},{4,7},{5,6},{6,5},{7,4},{8,11},{9,10},{10,... | collective-permute-start | bytes 221192 | tf_op jit(solution)/shard_map/ppermute | solution.py:278
  76.6 1.6 collective-permute-done.16.c3.refs_3_
  79.1 1.6 collective-permute-start.52
  82.0 3.9 %collective-permute-done.52 = f32[72,512]{1,0:T(8,128)S(1)} collective-permute-done((f32[72,512]{1,0:T(8,128)S(1)}, f32[72,512]{1,0:T(8,128)S(1)}, u32[]{:S(2)}, u32[]{:S(2)}) %collective-permute-start.52) | collective-permute-done | bytes 147488 | tf_op jit(solution)/shard_map/ppermute | solution.py:278
  86.3 2.3 %collective-permute-done.18 = f32[72,512]{1,0:T(8,128)S(1)} collective-permute-done((f32[72,512]{1,0:T(8,128)S(1)}, f32[72,512]{1,0:T(8,128)S(1)}, u32[]{:S(2)}, u32[]{:S(2)}) %collective-permute-start.18) | collective-permute-done | bytes 147488 | tf_op jit(solution)/shard_map/ppermute | solution.py:278
  89.9 2.2 %collective-permute-start.54 = (f32[72,256]{1,0:T(8,128)S(1)}, f32[72,256]{1,0:T(8,128)S(1)}, u32[]{:S(2)}, u32[]{:S(2)}) collective-permute-start(f32[72,256]{1,0:T(8,128)S(1)} %get-tuple-element.145), channel_id=1, source_target_pairs={{0,3},{1,2},{2,1},{3,0},{4,7},{5,6},{6,5},{7,4},{8,11},{9,10},{10,... | collective-permute-start | bytes 221192 | tf_op jit(solution)/shard_map/ppermute | solution.py:278
  94.5 2.2 %collective-permute-start.20 = (f32[72,256]{1,0:T(8,128)S(1)}, f32[72,256]{1,0:T(8,128)S(1)}, u32[]{:S(2)}, u32[]{:S(2)}) collective-permute-start(f32[72,256]{1,0:T(8,128)S(1)} %get-tuple-element.157), channel_id=1, source_target_pairs={{0,3},{1,2},{2,1},{3,0},{4,7},{5,6},{6,5},{7,4},{8,11},{9,10},{10,... | collective-permute-start | bytes 221192 | tf_op jit(solution)/shard_map/ppermute | solution.py:278
  98.1 2.0 %collective-permute-start.57 = (f32[72,256]{1,0:T(8,128)S(1)}, f32[72,256]{1,0:T(8,128)S(1)}, u32[]{:S(2)}, u32[]{:S(2)}) collective-permute-start(f32[72,256]{1,0:T(8,128)S(1)} %fusion.12.here_ref), channel_id=1, source_target_pairs={{0,4},{1,5},{2,6},{3,7},{4,0},{5,1},{6,2},{7,3},{8,12},{9,13},{10,... | collective-permute-start | bytes 221192 | tf_op jit(solution)/shard_map/ppermute | solution.py:278
  101.9 1.7 %collective-permute-start.23 = (f32[72,256]{1,0:T(8,128)S(1)}, f32[72,256]{1,0:T(8,128)S(1)}, u32[]{:S(2)}, u32[]{:S(2)}) collective-permute-start(f32[72,256]{1,0:T(8,128)S(1)} %fusion.20.here_ref), channel_id=1, source_target_pairs={{0,4},{1,5},{2,6},{3,7},{4,0},{5,1},{6,2},{7,3},{8,12},{9,13},{10,... | collective-permute-start | bytes 221192 | tf_op jit(solution)/shard_map/ppermute | solution.py:278
  105.3 1.9 %collective-permute-start.59 = (f32[72,256]{1,0:T(8,128)S(1)}, f32[72,256]{1,0:T(8,128)S(1)}, u32[]{:S(2)}, u32[]{:S(2)}) collective-permute-start(f32[72,256]{1,0:T(8,128)S(1)} %get-tuple-element.114.c0.refs_0_), channel_id=1, source_target_pairs={{0,2},{1,3},{2,0},{3,1},{4,6},{5,7},{6,4},{7,5},{8,10},{9,11},{10,... | collective-permute-start | bytes 221192 | tf_op jit(solution)/shard_map/ppermute | solution.py:278
  114.1 2.3 %collective-permute-done.26.c3.refs_3_ = f32[72,256]{1,0:T(8,128)S(1)} collective-permute-done((f32[72,256]{1,0:T(8,128)S(1)}, f32[72,256]{1,0:T(8,128)S(1)}, u32[]{:S(2)}, u32[]{:S(2)}) %collective-permute-start.26) | collective-permute-done | bytes 73760 | tf_op jit(solution)/shard_map/ppermute | solution.py:278
  117.3 1.6 collective-permute-start.62
  120.2 3.9 %collective-permute-done.62 = f32[72,512]{1,0:T(8,128)S(1)} collective-permute-done((f32[72,512]{1,0:T(8,128)S(1)}, f32[72,512]{1,0:T(8,128)S(1)}, u32[]{:S(2)}, u32[]{:S(2)}) %collective-permute-start.62) | collective-permute-done | bytes 147488 | tf_op jit(solution)/shard_map/ppermute | solution.py:278
  124.5 2.3 %collective-permute-done.28 = f32[72,512]{1,0:T(8,128)S(1)} collective-permute-done((f32[72,512]{1,0:T(8,128)S(1)}, f32[72,512]{1,0:T(8,128)S(1)}, u32[]{:S(2)}, u32[]{:S(2)}) %collective-permute-start.28) | collective-permute-done | bytes 147488 | tf_op jit(solution)/shard_map/ppermute | solution.py:278
  136.1 3.3 %collective-permute-start.67 = (f32[72,256]{1,0:T(8,128)S(1)}, f32[72,256]{1,0:T(8,128)S(1)}, u32[]{:S(2)}, u32[]{:S(2)}) collective-permute-start(f32[72,256]{1,0:T(8,128)S(1)} %fusion.10.here_ref), channel_id=1, source_target_pairs={{0,4},{1,5},{2,6},{3,7},{4,0},{5,1},{6,2},{7,3},{8,12},{9,13},{10,... | collective-permute-start | bytes 221192 | tf_op jit(solution)/shard_map/ppermute | solution.py:278
  139.5 2.9 %collective-permute-start.33 = (f32[72,256]{1,0:T(8,128)S(1)}, f32[72,256]{1,0:T(8,128)S(1)}, u32[]{:S(2)}, u32[]{:S(2)}) collective-permute-start(f32[72,256]{1,0:T(8,128)S(1)} %fusion.18.here_ref), channel_id=1, source_target_pairs={{0,4},{1,5},{2,6},{3,7},{4,0},{5,1},{6,2},{7,3},{8,12},{9,13},{10,... | collective-permute-start | bytes 221192 | tf_op jit(solution)/shard_map/ppermute | solution.py:278
  148.1 2.1 %collective-permute-start.70 = (f32[72,256]{1,0:T(8,128)S(1)}, f32[72,256]{1,0:T(8,128)S(1)}, u32[]{:S(2)}, u32[]{:S(2)}) collective-permute-start(f32[72,256]{1,0:T(8,128)S(1)} %get-tuple-element.123.refs_10_), channel_id=1, source_target_pairs={{0,3},{1,2},{2,1},{3,0},{4,7},{5,6},{6,5},{7,4},{8,11},{9,10},{10,... | collective-permute-start | bytes 221192 | tf_op jit(solution)/shard_map/ppermute | solution.py:278
  (209 shorter events, 78.5 us)
Async XLA Ops:
  9.1 9.5 %collective-permute-start.34 = (f32[72,256]{1,0:T(8,128)S(1)}, f32[72,256]{1,0:T(8,128)S(1)}, u32[]{:S(2)}, u32[]{:S(2)}) collective-permute-start(f32[72,256]{1,0:T(8,128)S(1)} %get-tuple-element.151), channel_id=1, source_target_pairs={{0,3},{1,2},{2,1},{3,0},{4,7},{5,6},{6,5},{7,4},{8,11},{9,10},{10,... | collective-permute-start | bytes 221192 | tf_op jit(solution)/shard_map/ppermute | solution.py:278
  14.7 7.1 %collective-permute-start = (f32[72,256]{1,0:T(8,128)S(1)}, f32[72,256]{1,0:T(8,128)S(1)}, u32[]{:S(2)}, u32[]{:S(2)}) collective-permute-start(f32[72,256]{1,0:T(8,128)S(1)} %get-tuple-element.163), channel_id=1, source_target_pairs={{0,3},{1,2},{2,1},{3,0},{4,7},{5,6},{6,5},{7,4},{8,11},{9,10},{10,... | collective-permute-start | bytes 221192 | tf_op jit(solution)/shard_map/ppermute | solution.py:278
  18.8 7.2 %collective-permute-start.37 = (f32[72,256]{1,0:T(8,128)S(1)}, f32[72,256]{1,0:T(8,128)S(1)}, u32[]{:S(2)}, u32[]{:S(2)}) collective-permute-start(f32[72,256]{1,0:T(8,128)S(1)} %fusion.16.here_ref), channel_id=1, source_target_pairs={{0,4},{1,5},{2,6},{3,7},{4,0},{5,1},{6,2},{7,3},{8,12},{9,13},{10,... | collective-permute-start | bytes 221192 | tf_op jit(solution)/shard_map/ppermute | solution.py:278
  23.0 8.0 %collective-permute-start.3 = (f32[72,256]{1,0:T(8,128)S(1)}, f32[72,256]{1,0:T(8,128)S(1)}, u32[]{:S(2)}, u32[]{:S(2)}) collective-permute-start(f32[72,256]{1,0:T(8,128)S(1)} %fusion.8.here_ref), channel_id=1, source_target_pairs={{0,4},{1,5},{2,6},{3,7},{4,0},{5,1},{6,2},{7,3},{8,12},{9,13},{10,... | collective-permute-start | bytes 221192 | tf_op jit(solution)/shard_map/ppermute | solution.py:278
  26.3 8.0 %collective-permute-start.38 = (f32[72,256]{1,0:T(8,128)S(1)}, f32[72,256]{1,0:T(8,128)S(1)}, u32[]{:S(2)}, u32[]{:S(2)}) collective-permute-start(f32[72,256]{1,0:T(8,128)S(1)} %get-tuple-element.102.c0.refs_0_), channel_id=1, source_target_pairs={{0,1},{1,0},{2,3},{3,2},{4,5},{5,4},{6,7},{7,6},{8,9},{9,8},{10,11... | collective-permute-start | bytes 221192 | tf_op jit(solution)/shard_map/ppermute | solution.py:278
  27.8 7.1 %collective-permute-start.39 = (f32[72,256]{1,0:T(8,128)S(1)}, f32[72,256]{1,0:T(8,128)S(1)}, u32[]{:S(2)}, u32[]{:S(2)}) collective-permute-start(f32[72,256]{1,0:T(8,128)S(1)} %get-tuple-element.102.c0.refs_0_), channel_id=1, source_target_pairs={{0,2},{1,3},{2,0},{3,1},{4,6},{5,7},{6,4},{7,5},{8,10},{9,11},{10,... | collective-permute-start | bytes 221192 | tf_op jit(solution)/shard_map/ppermute | solution.py:278
  40.6 6.8 %collective-permute-start.42 = (f32[72,512]{1,0:T(8,128)S(1)}, f32[72,512]{1,0:T(8,128)S(1)}, u32[]{:S(2)}, u32[]{:S(2)}) collective-permute-start(f32[72,512]{1,0:T(8,128)S(1)} %fusion.2), channel_id=1, source_target_pairs={{0,16},{1,17},{2,18},{3,19},{4,20},{5,21},{6,22},{7,23},{8,24},{9,... | collective-permute-start | bytes 442376 | tf_op jit(solution)/shard_map/ppermute | solution.py:278
  42.2 7.9 %collective-permute-start.8 = (f32[72,512]{1,0:T(8,128)S(1)}, f32[72,512]{1,0:T(8,128)S(1)}, u32[]{:S(2)}, u32[]{:S(2)}) collective-permute-start(f32[72,512]{1,0:T(8,128)S(1)} %fusion.5), channel_id=1, source_target_pairs={{0,16},{1,17},{2,18},{3,19},{4,20},{5,21},{6,22},{7,23},{8,24},{9,... | collective-permute-start | bytes 442376 | tf_op jit(solution)/shard_map/ppermute | solution.py:278
  51.2 6.6 %collective-permute-start.44 = (f32[72,256]{1,0:T(8,128)S(1)}, f32[72,256]{1,0:T(8,128)S(1)}, u32[]{:S(2)}, u32[]{:S(2)}) collective-permute-start(f32[72,256]{1,0:T(8,128)S(1)} %get-tuple-element.148), channel_id=1, source_target_pairs={{0,3},{1,2},{2,1},{3,0},{4,7},{5,6},{6,5},{7,4},{8,11},{9,10},{10,... | collective-permute-start | bytes 221192 | tf_op jit(solution)/shard_map/ppermute | solution.py:278
  52.0 7.3 %collective-permute-start.45 = (f32[72,256]{1,0:T(8,128)S(1)}, f32[72,256]{1,0:T(8,128)S(1)}, u32[]{:S(2)}, u32[]{:S(2)}) collective-permute-start(f32[72,256]{1,0:T(8,128)S(1)} %get-tuple-element.150), channel_id=1, source_target_pairs={{0,1},{1,0},{2,3},{3,2},{4,5},{5,4},{6,7},{7,6},{8,9},{9,8},{10,11... | collective-permute-start | bytes 221192 | tf_op jit(solution)/shard_map/ppermute | solution.py:278
  55.7 7.1 %collective-permute-start.10 = (f32[72,256]{1,0:T(8,128)S(1)}, f32[72,256]{1,0:T(8,128)S(1)}, u32[]{:S(2)}, u32[]{:S(2)}) collective-permute-start(f32[72,256]{1,0:T(8,128)S(1)} %get-tuple-element.160), channel_id=1, source_target_pairs={{0,3},{1,2},{2,1},{3,0},{4,7},{5,6},{6,5},{7,4},{8,11},{9,10},{10,... | collective-permute-start | bytes 221192 | tf_op jit(solution)/shard_map/ppermute | solution.py:278
  59.3 7.8 %collective-permute-start.47 = (f32[72,256]{1,0:T(8,128)S(1)}, f32[72,256]{1,0:T(8,128)S(1)}, u32[]{:S(2)}, u32[]{:S(2)}) collective-permute-start(f32[72,256]{1,0:T(8,128)S(1)} %fusion.14.here_ref), channel_id=1, source_target_pairs={{0,4},{1,5},{2,6},{3,7},{4,0},{5,1},{6,2},{7,3},{8,12},{9,13},{10,... | collective-permute-start | bytes 221192 | tf_op jit(solution)/shard_map/ppermute | solution.py:278
  62.9 8.2 %collective-permute-start.13 = (f32[72,256]{1,0:T(8,128)S(1)}, f32[72,256]{1,0:T(8,128)S(1)}, u32[]{:S(2)}, u32[]{:S(2)}) collective-permute-start(f32[72,256]{1,0:T(8,128)S(1)} %fusion.22.here_ref), channel_id=1, source_target_pairs={{0,4},{1,5},{2,6},{3,7},{4,0},{5,1},{6,2},{7,3},{8,12},{9,13},{10,... | collective-permute-start | bytes 221192 | tf_op jit(solution)/shard_map/ppermute | solution.py:278
  67.6 7.4 %collective-permute-start.49 = (f32[72,256]{1,0:T(8,128)S(1)}, f32[72,256]{1,0:T(8,128)S(1)}, u32[]{:S(2)}, u32[]{:S(2)}) collective-permute-start(f32[72,256]{1,0:T(8,128)S(1)} %get-tuple-element.107.c0.refs_0_), channel_id=1, source_target_pairs={{0,2},{1,3},{2,0},{3,1},{4,6},{5,7},{6,4},{7,5},{8,10},{9,11},{10,... | collective-permute-start | bytes 221192 | tf_op jit(solution)/shard_map/ppermute | solution.py:278
  68.5 7.1 %collective-permute-start.50 = (f32[72,256]{1,0:T(8,128)S(1)}, f32[72,256]{1,0:T(8,128)S(1)}, u32[]{:S(2)}, u32[]{:S(2)}) collective-permute-start(f32[72,256]{1,0:T(8,128)S(1)} %get-tuple-element.107.c0.refs_0_), channel_id=1, source_target_pairs={{0,3},{1,2},{2,1},{3,0},{4,7},{5,6},{6,5},{7,4},{8,11},{9,10},{10,... | collective-permute-start | bytes 221192 | tf_op jit(solution)/shard_map/ppermute | solution.py:278
  79.1 6.8 %collective-permute-start.52 = (f32[72,512]{1,0:T(8,128)S(1)}, f32[72,512]{1,0:T(8,128)S(1)}, u32[]{:S(2)}, u32[]{:S(2)}) collective-permute-start(f32[72,512]{1,0:T(8,128)S(1)} %fusion.1), channel_id=1, source_target_pairs={{0,16},{1,17},{2,18},{3,19},{4,20},{5,21},{6,22},{7,23},{8,24},{9,... | collective-permute-start | bytes 442376 | tf_op jit(solution)/shard_map/ppermute | solution.py:278
  80.7 7.9 %collective-permute-start.18 = (f32[72,512]{1,0:T(8,128)S(1)}, f32[72,512]{1,0:T(8,128)S(1)}, u32[]{:S(2)}, u32[]{:S(2)}) collective-permute-start(f32[72,512]{1,0:T(8,128)S(1)} %fusion.4), channel_id=1, source_target_pairs={{0,16},{1,17},{2,18},{3,19},{4,20},{5,21},{6,22},{7,23},{8,24},{9,... | collective-permute-start | bytes 442376 | tf_op jit(solution)/shard_map/ppermute | solution.py:278
  89.9 6.9 %collective-permute-start.54 = (f32[72,256]{1,0:T(8,128)S(1)}, f32[72,256]{1,0:T(8,128)S(1)}, u32[]{:S(2)}, u32[]{:S(2)}) collective-permute-start(f32[72,256]{1,0:T(8,128)S(1)} %get-tuple-element.145), channel_id=1, source_target_pairs={{0,3},{1,2},{2,1},{3,0},{4,7},{5,6},{6,5},{7,4},{8,11},{9,10},{10,... | collective-permute-start | bytes 221192 | tf_op jit(solution)/shard_map/ppermute | solution.py:278
  98.1 6.3 %collective-permute-start.57 = (f32[72,256]{1,0:T(8,128)S(1)}, f32[72,256]{1,0:T(8,128)S(1)}, u32[]{:S(2)}, u32[]{:S(2)}) collective-permute-start(f32[72,256]{1,0:T(8,128)S(1)} %fusion.12.here_ref), channel_id=1, source_target_pairs={{0,4},{1,5},{2,6},{3,7},{4,0},{5,1},{6,2},{7,3},{8,12},{9,13},{10,... | collective-permute-start | bytes 221192 | tf_op jit(solution)/shard_map/ppermute | solution.py:278
  101.9 6.4 %collective-permute-start.23 = (f32[72,256]{1,0:T(8,128)S(1)}, f32[72,256]{1,0:T(8,128)S(1)}, u32[]{:S(2)}, u32[]{:S(2)}) collective-permute-start(f32[72,256]{1,0:T(8,128)S(1)} %fusion.20.here_ref), channel_id=1, source_target_pairs={{0,4},{1,5},{2,6},{3,7},{4,0},{5,1},{6,2},{7,3},{8,12},{9,13},{10,... | collective-permute-start | bytes 221192 | tf_op jit(solution)/shard_map/ppermute | solution.py:278
  105.3 7.0 %collective-permute-start.59 = (f32[72,256]{1,0:T(8,128)S(1)}, f32[72,256]{1,0:T(8,128)S(1)}, u32[]{:S(2)}, u32[]{:S(2)}) collective-permute-start(f32[72,256]{1,0:T(8,128)S(1)} %get-tuple-element.114.c0.refs_0_), channel_id=1, source_target_pairs={{0,2},{1,3},{2,0},{3,1},{4,6},{5,7},{6,4},{7,5},{8,10},{9,11},{10,... | collective-permute-start | bytes 221192 | tf_op jit(solution)/shard_map/ppermute | solution.py:278
  117.3 6.8 %collective-permute-start.62 = (f32[72,512]{1,0:T(8,128)S(1)}, f32[72,512]{1,0:T(8,128)S(1)}, u32[]{:S(2)}, u32[]{:S(2)}) collective-permute-start(f32[72,512]{1,0:T(8,128)S(1)} %fusion), channel_id=1, source_target_pairs={{0,16},{1,17},{2,18},{3,19},{4,20},{5,21},{6,22},{7,23},{8,24},{9,... | collective-permute-start | bytes 442376 | tf_op jit(solution)/shard_map/ppermute | solution.py:278
  118.9 7.9 %collective-permute-start.28 = (f32[72,512]{1,0:T(8,128)S(1)}, f32[72,512]{1,0:T(8,128)S(1)}, u32[]{:S(2)}, u32[]{:S(2)}) collective-permute-start(f32[72,512]{1,0:T(8,128)S(1)} %fusion.3), channel_id=1, source_target_pairs={{0,16},{1,17},{2,18},{3,19},{4,20},{5,21},{6,22},{7,23},{8,24},{9,... | collective-permute-start | bytes 442376 | tf_op jit(solution)/shard_map/ppermute | solution.py:278
  127.9 6.8 %collective-permute-start.64 = (f32[72,256]{1,0:T(8,128)S(1)}, f32[72,256]{1,0:T(8,128)S(1)}, u32[]{:S(2)}, u32[]{:S(2)}) collective-permute-start(f32[72,256]{1,0:T(8,128)S(1)} %get-tuple-element.142), channel_id=1, source_target_pairs={{0,3},{1,2},{2,1},{3,0},{4,7},{5,6},{6,5},{7,4},{8,11},{9,10},{10,... | collective-permute-start | bytes 221192 | tf_op jit(solution)/shard_map/ppermute | solution.py:278
  129.2 6.9 %collective-permute-start.65 = (f32[72,256]{1,0:T(8,128)S(1)}, f32[72,256]{1,0:T(8,128)S(1)}, u32[]{:S(2)}, u32[]{:S(2)}) collective-permute-start(f32[72,256]{1,0:T(8,128)S(1)} %get-tuple-element.144), channel_id=1, source_target_pairs={{0,1},{1,0},{2,3},{3,2},{4,5},{5,4},{6,7},{7,6},{8,9},{9,8},{10,11... | collective-permute-start | bytes 221192 | tf_op jit(solution)/shard_map/ppermute | solution.py:278
  132.5 6.9 %collective-permute-start.30 = (f32[72,256]{1,0:T(8,128)S(1)}, f32[72,256]{1,0:T(8,128)S(1)}, u32[]{:S(2)}, u32[]{:S(2)}) collective-permute-start(f32[72,256]{1,0:T(8,128)S(1)} %get-tuple-element.154), channel_id=1, source_target_pairs={{0,3},{1,2},{2,1},{3,0},{4,7},{5,6},{6,5},{7,4},{8,11},{9,10},{10,... | collective-permute-start | bytes 221192 | tf_op jit(solution)/shard_map/ppermute | solution.py:278
  136.1 7.8 %collective-permute-start.67 = (f32[72,256]{1,0:T(8,128)S(1)}, f32[72,256]{1,0:T(8,128)S(1)}, u32[]{:S(2)}, u32[]{:S(2)}) collective-permute-start(f32[72,256]{1,0:T(8,128)S(1)} %fusion.10.here_ref), channel_id=1, source_target_pairs={{0,4},{1,5},{2,6},{3,7},{4,0},{5,1},{6,2},{7,3},{8,12},{9,13},{10,... | collective-permute-start | bytes 221192 | tf_op jit(solution)/shard_map/ppermute | solution.py:278
  139.5 6.5 %collective-permute-start.33 = (f32[72,256]{1,0:T(8,128)S(1)}, f32[72,256]{1,0:T(8,128)S(1)}, u32[]{:S(2)}, u32[]{:S(2)}) collective-permute-start(f32[72,256]{1,0:T(8,128)S(1)} %fusion.18.here_ref), channel_id=1, source_target_pairs={{0,4},{1,5},{2,6},{3,7},{4,0},{5,1},{6,2},{7,3},{8,12},{9,13},{10,... | collective-permute-start | bytes 221192 | tf_op jit(solution)/shard_map/ppermute | solution.py:278
  148.1 6.6 %collective-permute-start.70 = (f32[72,256]{1,0:T(8,128)S(1)}, f32[72,256]{1,0:T(8,128)S(1)}, u32[]{:S(2)}, u32[]{:S(2)}) collective-permute-start(f32[72,256]{1,0:T(8,128)S(1)} %get-tuple-element.123.refs_10_), channel_id=1, source_target_pairs={{0,3},{1,2},{2,1},{3,0},{4,7},{5,6},{6,5},{7,4},{8,11},{9,10},{10,... | collective-permute-start | bytes 221192 | tf_op jit(solution)/shard_map/ppermute | solution.py:278
  150.2 9.3 %collective-permute-start.73 = (f32[72,256]{1,0:T(8,128)S(1)}, f32[72,256]{1,0:T(8,128)S(1)}, u32[]{:S(2)}, u32[]{:S(2)}) collective-permute-start(f32[72,256]{1,0:T(8,128)S(1)} %get-tuple-element.122.refs_2_), channel_id=1, source_target_pairs={{0,1},{1,0},{2,3},{3,2},{4,5},{5,4},{6,7},{7,6},{8,9},{9,8},{10,11... | collective-permute-start | bytes 221192 | tf_op jit(solution)/shard_map/ppermute | solution.py:278
  151.4 8.1 %collective-permute-start.74 = (f32[72,256]{1,0:T(8,128)S(1)}, f32[72,256]{1,0:T(8,128)S(1)}, u32[]{:S(2)}, u32[]{:S(2)}) collective-permute-start(f32[72,256]{1,0:T(8,128)S(1)} %get-tuple-element.122.refs_2_), channel_id=1, source_target_pairs={{0,2},{1,3},{2,0},{3,1},{4,6},{5,7},{6,4},{7,5},{8,10},{9,11},{10,... | collective-permute-start | bytes 221192 | tf_op jit(solution)/shard_map/ppermute | solution.py:278
  152.5 7.0 %collective-permute-start.75 = (f32[72,256]{1,0:T(8,128)S(1)}, f32[72,256]{1,0:T(8,128)S(1)}, u32[]{:S(2)}, u32[]{:S(2)}) collective-permute-start(f32[72,256]{1,0:T(8,128)S(1)} %get-tuple-element.122.refs_2_), channel_id=1, source_target_pairs={{0,3},{1,2},{2,1},{3,0},{4,7},{5,6},{6,5},{7,4},{8,11},{9,10},{10,... | collective-permute-start | bytes 221192 | tf_op jit(solution)/shard_map/ppermute | solution.py:278
  (51 other events, 252.0 us)
